TPU v7x, 32 devices: a whole 2x2x4 slice. The times are simulated.
32 devices in a mesh: grp: 2 (over x), pi: 16 (over z, y, core).
Axes of the slice: x: 2, y: 2, z: 4, core: 2. Of those that a mesh axis runs over, the one named last changes fastest.
Arguments:
- left: bfloat16 [128, 1024], P(('grp', 'pi')), parts along dimension 0, may hold values from -6 to 6
- right: bfloat16 [128, 1024], P(('grp', 'pi')), parts along dimension 0, may hold values from -6 to 6
- depth: int32 [128], P(('grp', 'pi')), parts along dimension 0, may hold values from 1 to 32
- w_out: bfloat16 [1024, 128], replicated, may hold values from -0.1875 to 0.1875
- bias: float32 [128], replicated, may hold values from -4 to 4
- pair_cot: bfloat16 [128, 64, 128], P(('grp', 'pi')), parts along dimension 0, may hold values from -6 to 6
Outputs:
- pair_update: bfloat16 [128, 64, 128], P(('grp', 'pi')), parts along dimension 0
- grad_left: float32 [128, 1024], P(('grp', 'pi')), parts along dimension 0
- grad_right: float32 [128, 1024], P(('grp', 'pi')), parts along dimension 0
- grad_w: float32 [2048, 128], P('grp'), parts along dimension 0
- grad_bias: float32 [256], P('grp'), parts along dimension 0
There are 2 independent parts, one for each index of `grp`. A program takes and returns all parts, laid end to end along the dimension named above; an argument that names none is the same for every part. Nothing has to cross between parts.
All inputs are finite; a program needn't handle non-finite values.
Results may differ from a plain program's by a relative error of at most 0.0034.
Values may be sent and summed in bfloat16 or wider, within the bound.
A program may use at most 64 MiB of HBM per device.

v0:
```python
import math

import jax
import jax.numpy as jnp
from jax import lax
from jax.sharding import PartitionSpec as P

C = 32


epsilon = 0.001


def local(left, right, depth, w_out, bias, pair_cot):
    rows = left.shape[0]
    width = left.shape[1]
    alignment = width // C
    total = pair_cot.shape[1]
    channels = w_out.shape[1]
    row_ids = jnp.arange(alignment, dtype=jnp.int32)
    own_mask = (row_ids[None, :] < depth[:, None]).astype(jnp.bfloat16)
    own_left = left.reshape(rows, alignment, C) * own_mask[:, :, None]
    w_back = w_out.T
    pair_cols = lax.all_to_all(pair_cot, "pi", split_axis=1, concat_axis=0, tiled=True)
    init = (
        jnp.zeros((rows, total, channels), jnp.bfloat16),
        jnp.zeros((rows, width), jnp.float32),
        jnp.zeros((C * C, channels), jnp.float32),
        jnp.zeros((channels,), jnp.float32),
    )
    carry = init
    start = jnp.int32(0)
    right_piece = lax.all_gather(right, "pi", axis=0, tiled=True)
    depth_piece = lax.all_gather(depth, "pi", axis=0, tiled=True)
    length = right_piece.shape[0]
    block = math.gcd(length, 256)
    for offset in range(0, length, block):
        begin = start + offset
        depth_block = depth_piece[offset : offset + block]
        mask_block = (row_ids[None, :] < depth_block[:, None]).astype(jnp.bfloat16)
        right_block = (
            right_piece[offset : offset + block].reshape(block, alignment, C)
            * mask_block[:, :, None]
        )
        count = epsilon + jnp.minimum(depth[:, None], depth_block[None, :]).astype(jnp.float32)
        outer = jnp.einsum(
            "isc,jsd->ijcd", own_left, right_block, preferred_element_type=jnp.float32
        )
        outer = (outer / count[:, :, None, None]).reshape(rows, block, C * C).astype(jnp.bfloat16)
        update = (jnp.dot(outer, w_out, preferred_element_type=jnp.float32) + bias).astype(
            jnp.bfloat16
        )
        cot_block = lax.dynamic_slice_in_dim(pair_cot, begin, block, 1)
        pair_out = lax.dynamic_update_slice(carry[0], update, (0, begin, 0))
        weight_acc = carry[2] + jnp.dot(
            outer.reshape(-1, C * C).T,
            cot_block.reshape(-1, channels),
            preferred_element_type=jnp.float32,
        )
        bias_acc = carry[3] + jnp.sum(cot_block, axis=(0, 1), dtype=jnp.float32)
        grad_pair = (
            jnp.dot(cot_block, w_back, preferred_element_type=jnp.float32) / count[:, :, None]
        )
        grad_pair = grad_pair.astype(jnp.bfloat16).reshape(rows, block, C, C)
        left_acc = carry[1] + jnp.einsum(
            "ijcd,jsd->isc", grad_pair, right_block, preferred_element_type=jnp.float32
        ).reshape(rows, width)
        carry = (pair_out, left_acc, weight_acc, bias_acc)
    pair_update = carry[0]
    left_acc = carry[1]
    accum = jnp.zeros((rows, width), jnp.float32)
    start = jnp.int32(0)
    left_piece = lax.all_gather(left, "pi", axis=0, tiled=True)
    depth_piece = lax.all_gather(depth, "pi", axis=0, tiled=True)
    length = left_piece.shape[0]
    block = math.gcd(length, 256)
    for offset in range(0, length, block):
        begin = start + offset
        depth_block = depth_piece[offset : offset + block]
        mask_block = (row_ids[None, :] < depth_block[:, None]).astype(jnp.bfloat16)
        left_block = (
            left_piece[offset : offset + block].reshape(block, alignment, C)
            * mask_block[:, :, None]
        )
        count = epsilon + jnp.minimum(depth_block[:, None], depth[None, :]).astype(jnp.float32)
        cot_block = lax.dynamic_slice_in_dim(pair_cols, begin, block, 0)
        grad_pair = (
            jnp.dot(cot_block, w_back, preferred_element_type=jnp.float32) / count[:, :, None]
        )
        grad_pair = grad_pair.astype(jnp.bfloat16).reshape(block, rows, C, C)
        accum = accum + jnp.einsum(
            "ijcd,isc->jsd", grad_pair, left_block, preferred_element_type=jnp.float32
        ).reshape(rows, width)
    grad_w, grad_bias = lax.psum((carry[2], carry[3]), "pi")
    grad_left = (left_acc.reshape(rows, alignment, C) * own_mask[:, :, None]).reshape(rows, width)
    grad_right = (accum.reshape(rows, alignment, C) * own_mask[:, :, None]).reshape(rows, width)
    return (pair_update, grad_left, grad_right, grad_w, grad_bias)


def solution(mesh):
    placed = (
        P(("grp", "pi"), None),
        P(("grp", "pi"), None),
        P(("grp", "pi")),
        P(),
        P(),
        P(("grp", "pi"), None, None),
    )
    return jax.shard_map(
        local,
        mesh=mesh,
        in_specs=placed,
        out_specs=(
            P(("grp", "pi"), None, None),
            P(("grp", "pi"), None),
            P(("grp", "pi"), None),
            P("grp", None),
            P("grp"),
        ),
        check_vma=False,
    )
```

profile of v0, /device:TPU:1, one launch (start us, length us, event | category | flops | bytes accessed | tf_op | source)
XLA Modules:
  0.0 146.0 jit_solution(4158764540035762436)
XLA Ops:
  7.2 1.3 dynamic-slice
  9.2 0.9 dynamic-update-slice
  10.0 10.7 %all-reduce = s32[64]{0:T(128)S(1)} all-reduce(s32[64]{0:T(128)S(1)} %dynamic-update-slice), channel_id=1, replica_groups=mesh['grp'=2,'pi'=16] {'pi'}, use_global_device_ids=true, to_apply=%add | all-reduce | flops 64 | bytes 512
  20.8 0.7 convert_add_fusion.1
  21.5 1.3 fusion.19
  22.8 21.4 %all-gather = bf16[16,4,1024]{2,1,0:T(4,128)(2,1)S(1)} all-gather(bf16[1,4,1024]{2,1,0:T(4,128)(2,1)} %bitcast.65), channel_id=1, replica_groups=mesh['grp'=2,'pi'=16] {'pi'}, dimensions={0}, use_global_device_ids=true | all-gather | bytes 139264 | tf_op jit(solution)/shard_map/all_gather | solution.py:33
  44.6 0.2 copy.45
  45.0 0.7 mul.54
  45.8 0.5 fusion
  46.3 0.7 copy.48
  47.1 1.2 convolution_bitcast_fusion
  48.3 0.7 copy.52
  49.0 4.0 %all-to-all-start = ((bf16[4,64,128]{2,0,1:T(4,128)(2,1)}), bf16[4,64,128]{2,0,1:T(4,128)(2,1)}, u32[]{:S(2)}, u32[]{:S(2)}) async-start(bf16[4,64,128]{2,0,1:T(4,128)(2,1)} %copy.52), calls=%async_computation | async-start | bytes 131072 | tf_op jit(solution)/shard_map/all_to_all | solution.py:24
  53.0 0.3 reshape.180
  53.3 0.6 convert_reduce_fusion
  53.9 0.3 fusion.1
  54.2 0.5 copy.50
  54.7 3.8 %copy.51 = bf16[4,64,32,32]{3,2,1,0:T(8,128)(2,1)} copy(bf16[4,64,32,32]{1,3,2,0:T(8,128)(2,1)S(1)} %bitcast.59) | data formatting | bytes 1048576 | tf_op jit(solution)/shard_map/reshape | solution.py:64
  58.5 2.9 %fusion.4 = f32[4,32,32]{2,1,0:T(8,128)S(1)} fusion(bf16[4,64,32,32]{3,2,1,0:T(8,128)(2,1)} %copy.51, bf16[64,32,32]{2,1,0:T(8,128)(2,1)S(1)} %reshape.180, bf16[64,32]{1,0:T(8,128)(2,1)S(1)} %fusion.17, f32[4,32]{1,0:T(4,128)S(1)} %copy-done.6), kind=kOutput, calls=%fused_computation.11 | convolution fusion | flops 17043456 | bytes 676352 | tf_op jit(solution)/shard_map/ijcd,jsd->isc/dot_general | solution.py:65
  61.4 0.7 reshape.182
  62.1 1.1 fusion.3
  63.2 22.1 %all-gather.1 = bf16[16,4,1024]{2,1,0:T(4,128)(2,1)S(1)} all-gather(bf16[1,4,1024]{2,1,0:T(4,128)(2,1)S(1)} %bitcast.64), channel_id=1, replica_groups=mesh['grp'=2,'pi'=16] {'pi'}, dimensions={0}, use_global_device_ids=true | all-gather | bytes 139264 | tf_op jit(solution)/shard_map/all_gather | solution.py:73
  85.3 1.1 reshape.183
  86.4 29.5 %psum.15 = f32[128]{0:T(128)} all-reduce(f32[128]{0:T(128)S(1)} %copy-done.9), channel_id=1, replica_groups=mesh['grp'=2,'pi'=16] {'pi'}, use_global_device_ids=true, to_apply=%region_2.0 | all-reduce | flops 128 | bytes 1024 | tf_op jit(solution)/shard_map/psum | solution.py:94
  116.0 0.9 copy.53
  116.8 0.3 fusion.2
  117.2 0.5 copy.54
  117.6 3.1 %copy.55 = bf16[64,4,32,32]{3,2,0,1:T(8,128)(2,1)S(1)} copy(bf16[64,4,32,32]{0,3,2,1:T(8,128)(2,1)S(1)} %bitcast.60) | data formatting | bytes 1048576 | tf_op jit(solution)/shard_map/reshape | solution.py:90
  120.7 1.9 %fusion.5 = f32[4,32,32]{2,1,0:T(8,128)S(1)} fusion(bf16[64,4,32,32]{3,2,0,1:T(8,128)(2,1)S(1)} %copy.55, bf16[64,32,32]{2,1,0:T(8,128)(2,1)} %reshape.183, bf16[64,32]{1,0:T(8,128)(2,1)S(1)} %fusion.17, f32[4,32]{1,0:T(4,128)S(1)} %copy-done.7), kind=kOutput, calls=%fused_computation.12 | convolution fusion | flops 17043456 | bytes 676352 | tf_op jit(solution)/shard_map/ijcd,isc->jsd/dot_general | solution.py:91
  122.7 0.7 reshape.185
  123.4 13.9 %all-reduce.3.cloned.1.call-done = f32[1024,128]{1,0:T(8,128)} async-done(((f32[1024,128]{1,0:T(8,128)}), f32[1024,128]{1,0:T(8,128)}) %all-reduce.3.cloned.1.call-update) | async-done | bytes 524304 | tf_op jit(solution)/shard_map/psum | solution.py:94
  137.3 1.9 %copy.71 = f32[1024,128]{1,0:T(8,128)} copy(f32[1024,128]{1,0:T(8,128)} %all-reduce.3.cloned.1.call-done) | data formatting | bytes 1048576
  (34 shorter events, 1.0 us)
Async XLA Ops:
  7.2 46.7 %copy-start = (bf16[1024,128]{1,0:T(8,128)(2,1)S(1)}, bf16[1024,128]{1,0:T(8,128)(2,1)}, u32[]{:S(2)}) copy-start(bf16[1024,128]{1,0:T(8,128)(2,1)} %param.9) | copy-start | bytes 786436
  7.2 130.1 %all-reduce.3.cloned.1.call-start = ((), (), s32[]{:S(2)}) async-start(), calls=%async_computation.1 | async-start | bytes 1048576 | tf_op jit(solution)/shard_map/psum | solution.py:94
  20.7 2.1 %copy-start.4 = (s32[64]{0:T(128)}, s32[64]{0:T(128)S(1)}, u32[]{:S(2)}) copy-start(s32[64]{0:T(128)S(1)} %all-reduce) | copy-start | bytes 772
  46.3 0.8 copy-start.1
  49.0 67.0 %all-to-all-start = ((bf16[4,64,128]{2,0,1:T(4,128)(2,1)}), bf16[4,64,128]{2,0,1:T(4,128)(2,1)}, u32[]{:S(2)}, u32[]{:S(2)}) async-start(bf16[4,64,128]{2,0,1:T(4,128)(2,1)} %copy.52), calls=%async_computation | async-start | bytes 131072 | tf_op jit(solution)/shard_map/all_to_all | solution.py:24
  54.2 4.3 %copy-start.6 = (f32[4,32]{1,0:T(4,128)S(1)}, f32[4,32]{1,0:T(4,128)}, u32[]{:S(2)}) copy-start(f32[4,32]{1,0:T(4,128)} %get-tuple-element.5) | copy-start | bytes 1540
  58.4 3.7 %copy-start.8 = (f32[128]{0:T(128)S(1)}, f32[128]{0:T(128)}, u32[]{:S(2)}) copy-start(f32[128]{0:T(128)} %param.10) | copy-start | bytes 1540
  58.4 4.7 %copy-start.2 = (bf16[4,1024]{1,0:T(4,128)(2,1)S(1)}, bf16[4,1024]{1,0:T(4,128)(2,1)}, u32[]{:S(2)}) copy-start(bf16[4,1024]{1,0:T(4,128)(2,1)} %param.6) | copy-start | bytes 24580
  58.5 27.9 %copy-start.9 = (f32[128]{0:T(128)S(1)}, f32[128]{0:T(128)}, u32[]{:S(2)}) copy-start(f32[128]{0:T(128)} %convert_reduce_fusion) | copy-start | bytes 1540
  58.5 57.4 %copy-start.3 = (s32[4]{0:T(128)S(1)}, s32[4]{0:T(128)}, u32[]{:S(2)}) copy-start(s32[4]{0:T(128)} %param.8) | copy-start | bytes 52
  58.5 57.4 %copy-start.5 = (s32[64]{0:T(128)S(1)}, s32[64]{0:T(128)}, u32[]{:S(2)}) copy-start(s32[64]{0:T(128)} %copy-done.4) | copy-start | bytes 772
  117.1 3.6 %copy-start.7 = (f32[4,32]{1,0:T(4,128)S(1)}, f32[4,32]{1,0:T(4,128)}, u32[]{:S(2)}) copy-start(f32[4,32]{1,0:T(4,128)} %get-tuple-element.5) | copy-start | bytes 1540
Sparse Core Ops, SparseCore 0:
  48.4 88.7 all-reduce.2
where the time goes:
time: 147 us; the launch traced here: 146 us
  blocking collectives  83.7 us (57%)
  local copies, waits for them, and re-layouts  17.7 us (12%)
  between operations  14.9 us (10%)
  waiting for transfers between devices  13.9 us (9%)
  matrix products  8.17 us (6%)
  starting transfers between devices  4.06 us (3%)
  other arithmetic  3.48 us (2%)
    psum x1, blocking collectives, local(): grad_w, grad_bias = lax.psum((carry[2], carry[3]), 'pi')  29.5 us
    all_gather x1, blocking collectives, local(): left_piece = lax.all_gather(left, 'pi', axis=0, tiled=True)  22.1 us
    all_gather x1, blocking collectives, local(): right_piece = lax.all_gather(right, 'pi', axis=0, tiled=True)  21.4 us
    psum x1, waiting for transfers between devices, local(): grad_w, grad_bias = lax.psum((carry[2], carry[3]), 'pi')  13.9 us
    unnamed x1, blocking collectives  10.7 us
    unnamed x27, local copies, waits for them, and re-layouts  4.99 us
    all_to_all x1, starting transfers between devices, local(): lax.all_to_all(pair_cot, 'pi', split_axis=1, concat_axis=0, tiled=True)  4.03 us
    reshape x1, local copies, waits for them, and re-layouts, local(): grad_pair = grad_pair.astype(jnp.bfloat16).reshape(rows, block, C, C)  3.77 us
  transfers between devices with their start and end apart: 2, of which 1 were waited for; matrix products, arithmetic and copies ran while one was open for 13% of the time, Pallas kernels for 0%

commit v1 on v0

v1 whole, which is shorter than its diff:
```python
import functools

import jax
import jax.numpy as jnp
from jax import lax
from jax.experimental import pallas as pl
from jax.experimental.pallas import tpu as pltpu
from jax.sharding import PartitionSpec as P

C = 32
EPSILON = 0.001
EXTRA = 16
MESH = pl.DeviceIdType.MESH
F32 = jnp.float32
BF16 = jnp.bfloat16


def split(x):
    high = x.astype(BF16)
    return high, (x - high.astype(F32)).astype(BF16)


def mm(x, y):
    return jnp.dot(x, y, preferred_element_type=F32)


def mm_nt(x, y):
    return lax.dot_general(x, y, (((1,), (1,)), ((), ())), preferred_element_type=F32)


def kernel(
    n, x_ref, a_ref, cot_ref, w_ref, bias_ref,
    pu_ref, gl_ref, gr_ref, gw_ref, gb_ref,
    gat, bs, uhi, ulo, t_ref, send_w, recv_w, part_r, send_r, recv_r, mine_w, all_w,
    send_sems, recv_sems,
):
    me = lax.axis_index("pi")
    rows = x_ref.shape[0]
    z = w_ref.shape[1]
    width = x_ref.shape[1] - z
    samples = width // C
    total = cot_ref.shape[1]
    chunk = gw_ref.shape[1]

    def copy(k, source, target, peer, slot):
        return pltpu.make_async_remote_copy(
            src_ref=source, dst_ref=target.at[slot],
            send_sem=send_sems.at[k, peer], recv_sem=recv_sems.at[k, slot],
            device_id={"pi": peer}, device_id_type=MESH,
        )

    def each(act):
        def body(step, carry):
            act(lax.rem(me + step, n))
            return carry

        lax.fori_loop(1, n, body, 0)

    barrier = pltpu.get_barrier_semaphore()
    each(lambda p: pl.semaphore_signal(barrier, inc=1, device_id={"pi": p}, device_id_type=MESH))
    pl.semaphore_wait(barrier, n - 1)
    each(lambda p: copy(0, x_ref, gat, p, me).start())
    gat[me] = x_ref[...]

    a = a_ref[...]
    for d in range(C):
        high, low = split(mm(a, w_ref[d * C:(d + 1) * C, :]))
        for i in range(rows):
            here = (slice(d * samples, (d + 1) * samples), slice(i * z, (i + 1) * z))
            uhi[here] = high[i * samples:(i + 1) * samples]
            ulo[here] = low[i * samples:(i + 1) * samples]
    a_t = jnp.concatenate([a, a], axis=0).astype(F32).T.astype(BF16)

    each(lambda p: copy(0, x_ref, gat, p, p).wait_recv())

    def gather_rows(q, carry):
        both = jnp.concatenate([gat[2 * q].astype(F32), gat[2 * q + 1].astype(F32)], axis=0)
        bs[pl.ds(pl.multiple_of(q * 2 * rows, 2 * rows), 2 * rows), :] = both
        return carry

    lax.fori_loop(0, n // 2, gather_rows, 0)
    b32 = bs[:, :width]
    b = b32.astype(BF16)
    depths = bs[:, width:]
    inverse, highs, lows = [], [], []
    cot_sum = jnp.zeros((1, z), F32)
    for i in range(rows):
        inverse.append(1.0 / (EPSILON + jnp.minimum(depths, x_ref[i:i + 1, width:].astype(F32))))
        cot = cot_ref[i].astype(F32)
        cot_sum = cot_sum + jnp.sum(cot, axis=0, keepdims=True)
        high, low = split(cot * inverse[i])
        highs.append(high)
        lows.append(low)
    cot_high = jnp.concatenate(highs, axis=1)
    cot_low = jnp.concatenate(lows, axis=1)
    b_t = jnp.concatenate([b32, b32], axis=0).T.astype(BF16)
    t_ref[...] = mm(b_t, jnp.concatenate([cot_high, cot_low], axis=0))

    def t_of(d):
        return jnp.concatenate(
            [t_ref[d * samples:(d + 1) * samples, i * z:(i + 1) * z] for i in range(rows)], axis=0
        )

    sum_high, sum_low = split(cot_sum)
    per = max(1, chunk // C)
    for d in range(C):
        high, low = split(t_of(d))
        piece = mm(a_t, jnp.concatenate([high, low], axis=0)).astype(BF16)
        if chunk >= C:
            send_w[d // per, (d % per) * C:(d % per + 1) * C, :] = piece
        else:
            for k in range(C // chunk):
                send_w[d * (C // chunk) + k, :chunk, :] = piece[k * chunk:(k + 1) * chunk]
    sums = jnp.concatenate(
        [sum_high.astype(F32), sum_low.astype(F32), jnp.zeros((EXTRA - 2, z), F32)], axis=0
    ).astype(BF16)

    def put_sums(p, carry):
        send_w[p, chunk:, :] = sums
        return carry

    lax.fori_loop(0, n, put_sums, 0)
    each(lambda p: copy(1, send_w.at[p], recv_w, p, me).start())
    recv_w[me] = send_w[me]

    u_high = uhi[...]
    part_r[...] = mm_nt(cot_high, u_high) + mm_nt(cot_low, u_high) + mm_nt(cot_high, ulo[...])

    def scatter_rows(q, carry):
        both = part_r[pl.ds(pl.multiple_of(q * 2 * rows, 2 * rows), 2 * rows), :]
        send_r[2 * q] = both[:rows].astype(BF16)
        send_r[2 * q + 1] = both[rows:].astype(BF16)
        return carry

    lax.fori_loop(0, n // 2, scatter_rows, 0)
    each(lambda p: copy(2, send_r.at[p], recv_r, p, me).start())
    recv_r[me] = send_r[me]

    each(lambda p: copy(1, send_w.at[p], recv_w, p, p).wait_recv())

    def add_w(p, acc):
        return acc + recv_w[p].astype(F32)

    total_w = lax.fori_loop(0, n, add_w, jnp.zeros((chunk + EXTRA, z), F32))
    mine_w[...] = total_w[:chunk].astype(BF16)
    gb_ref[...] = total_w[chunk:chunk + 1] + total_w[chunk + 1:chunk + 2]
    each(lambda p: copy(3, mine_w, all_w, p, me).start())
    all_w[me] = mine_w[...]

    update = mm(b, u_high) + mm(b, ulo[...])
    for i in range(rows):
        pu_ref[i] = (update[:, i * z:(i + 1) * z] * inverse[i] + bias_ref[...]).astype(BF16)

    left_acc = jnp.zeros((rows * samples, C), F32)
    for d in range(C):
        high, low = split(t_of(d))
        w_d = w_ref[d * C:(d + 1) * C, :]
        left_acc = left_acc + mm_nt(
            jnp.concatenate([high, low], axis=1), jnp.concatenate([w_d, w_d], axis=1)
        )
    gl_ref[...] = left_acc

    each(lambda p: copy(2, send_r.at[p], recv_r, p, p).wait_recv())

    def add_r(p, acc):
        return acc + recv_r[p].astype(F32)

    gr_ref[...] = lax.fori_loop(0, n, add_r, jnp.zeros((rows, width), F32))

    each(lambda p: copy(3, mine_w, all_w, p, p).wait_recv())
    gw_ref[...] = all_w[...]
    each(lambda p: copy(0, x_ref, gat, p, me).wait_send())
    each(lambda p: copy(1, send_w.at[p], recv_w, p, me).wait_send())
    each(lambda p: copy(2, send_r.at[p], recv_r, p, me).wait_send())
    each(lambda p: copy(3, mine_w, all_w, p, me).wait_send())


def local(n, left, right, depth, w_out, bias, pair_cot):
    rows, width = left.shape
    samples = width // C
    total, z = pair_cot.shape[1:]
    chunk = w_out.shape[0] // n
    mask = jnp.arange(samples, dtype=jnp.int32)[None, :] < depth[:, None]
    own = mask.astype(BF16)[:, :, None]
    a = (left.reshape(rows, samples, C) * own).reshape(rows * samples, C)
    b = (right.reshape(rows, samples, C) * own).transpose(0, 2, 1).reshape(rows, width)
    x = jnp.concatenate([b, jnp.broadcast_to(depth.astype(BF16)[:, None], (rows, z))], axis=1)
    w = w_out.reshape(C, C, z).transpose(1, 0, 2).reshape(C * C, z)
    vmem = pl.BlockSpec(memory_space=pltpu.VMEM)
    pu, gl, gr, gw, gb = pl.pallas_call(
        functools.partial(kernel, n),
        out_shape=(
            jax.ShapeDtypeStruct((rows, total, z), BF16),
            jax.ShapeDtypeStruct((rows * samples, C), F32),
            jax.ShapeDtypeStruct((rows, width), F32),
            jax.ShapeDtypeStruct((n, chunk, z), BF16),
            jax.ShapeDtypeStruct((1, z), F32),
        ),
        in_specs=[vmem] * 5,
        out_specs=(vmem,) * 5,
        scratch_shapes=[
            pltpu.VMEM((n, rows, width + z), BF16),
            pltpu.VMEM((total, width + z), F32),
            pltpu.VMEM((C * samples, rows * z), BF16),
            pltpu.VMEM((C * samples, rows * z), BF16),
            pltpu.VMEM((C * samples, rows * z), F32),
            pltpu.VMEM((n, chunk + EXTRA, z), BF16),
            pltpu.VMEM((n, chunk + EXTRA, z), BF16),
            pltpu.VMEM((total, width), F32),
            pltpu.VMEM((n, rows, width), BF16),
            pltpu.VMEM((n, rows, width), BF16),
            pltpu.VMEM((chunk, z), BF16),
            pltpu.VMEM((n, chunk, z), BF16),
            pltpu.SemaphoreType.DMA((4, n)),
            pltpu.SemaphoreType.DMA((4, n)),
        ],
        compiler_params=pltpu.CompilerParams(collective_id=0, has_side_effects=True),
    )(x, a, pair_cot, w, bias[None, :])
    grad_w = gw.astype(F32).reshape(C, C, z).transpose(1, 0, 2).reshape(C * C, z)
    keep = mask.astype(F32)
    grad_left = (gl.reshape(rows, samples, C) * keep[:, :, None]).reshape(rows, width)
    grad_right = (gr.reshape(rows, C, samples) * keep[:, None, :]).transpose(0, 2, 1).reshape(rows, width)
    return pu, grad_left, grad_right, grad_w, gb.reshape(z)


def solution(mesh):
    placed = (
        P(("grp", "pi"), None),
        P(("grp", "pi"), None),
        P(("grp", "pi")),
        P(),
        P(),
        P(("grp", "pi"), None, None),
    )
    return jax.shard_map(
        functools.partial(local, mesh.shape["pi"]),
        mesh=mesh,
        in_specs=placed,
        out_specs=(
            P(("grp", "pi"), None, None),
            P(("grp", "pi"), None),
            P(("grp", "pi"), None),
            P("grp", None),
            P("grp"),
        ),
        check_vma=False,
    )
```

time: 147 us -> 42.8 us (0.29)
  blocking collectives: 83.7 us -> 0 us
  Pallas kernels: 0 us -> 31.3 us
  between operations: 14.9 us -> 0.73 us
  waiting for transfers between devices: 13.9 us -> 0 us
  local copies, waits for them, and re-layouts: 17.7 us -> 7.07 us
  matrix products: 8.17 us -> 0 us
  starting transfers between devices: 4.06 us -> 0 us
    all_gather x2 -> x0, blocking collectives: 43.5 us -> none  [the longest x1 22.1 us: local(): left_piece = lax.all_gather(left, 'pi', axis=0, tiled=True)]
    pallas_call x0 -> x1, Pallas kernels: none -> 31.3 us  [local(): pl.pallas_call(functools.partial(kernel, n), out_shape=(jax.ShapeDtypeStr...]
    psum x1 -> x0, blocking collectives: 29.5 us -> none  [local(): grad_w, grad_bias = lax.psum((carry[2], carry[3]), 'pi')]
    psum x1 -> x0, waiting for transfers between devices: 13.9 us -> none  [local(): grad_w, grad_bias = lax.psum((carry[2], carry[3]), 'pi')]
    unnamed x1 -> x0, blocking collectives: 10.7 us -> none
    dot_general x7 -> x0, matrix products: 8.17 us -> none  [the longest x1 2.93 us: local(): jnp.einsum('ijcd,jsd->isc', grad_pair, right_block, preferred_element_typ...]
    reshape x6 -> x9, local copies, waits for them, and re-layouts: 9.61 us -> 5.45 us  [the longest x1 1.1 us: local(): gw.astype(F32).reshape(C, C, z).transpose(1, 0, 2).reshape(C * C, z)]
    all_to_all x1 -> x0, starting transfers between devices: 4.03 us -> none  [local(): lax.all_to_all(pair_cot, 'pi', split_axis=1, concat_axis=0, tiled=True)]
  transfers between devices with their start and end apart: 2 -> 0, of which waited for: 1 -> 0; matrix products, arithmetic and copies ran while one was open for 13% -> 0% of each run, Pallas kernels for 0% -> 0%
where the time goes in v1:
time: 42.8 us; the launch traced here: 42.5 us
  Pallas kernels  31.3 us (73%)
  local copies, waits for them, and re-layouts  7.07 us (17%)
  other arithmetic  3.42 us (8%)
  between operations  0.73 us (2%)
    pallas_call x1, Pallas kernels, local(): pl.pallas_call(functools.partial(kernel, n), out_shape=(jax.ShapeDtypeStr...  31.3 us
    unnamed x12, local copies, waits for them, and re-layouts  1.21 us
    reshape x1, local copies, waits for them, and re-layouts, local(): gw.astype(F32).reshape(C, C, z).transpose(1, 0, 2).reshape(C * C, z)  1.1 us
    reshape x1, local copies, waits for them, and re-layouts, local(): gl.reshape(rows, samples, C) * keep[:, :, None]  0.98 us
    reshape x2, local copies, waits for them, and re-layouts, local(): right.reshape(rows, samples, C) * own  0.88 us

profile of v1, /device:TPU:1, one launch (start us, length us, event | category | flops | bytes accessed | tf_op | source)
XLA Modules:
  0.0 42.5 jit_solution(2329504738917779473)
XLA Ops:
  0.6 0.0 copy-start.1
  0.6 0.7 %convert_element_type.29 = bf16[4]{0:T(256)(128)(2,1)S(1)} convert(s32[4]{0:T(128)} %param.8) | non-fusion elementwise | flops 4 | bytes 24 | tf_op jit(solution)/shard_map/convert_element_type | solution.py:187
  1.3 0.1 broadcast_in_dim.4
  1.4 0.7 %fusion = (f32[4,32]{1,0:T(4,128)S(1)}, bf16[4,32]{1,0:T(4,128)(2,1)S(1)}) fusion(s32[4]{0:T(128)} %param.8), kind=kLoop, calls=%fused_computation.6 | loop fusion | flops 384 | bytes 784 | tf_op jit(solution)/shard_map/convert_element_type | solution.py:220
  2.1 0.1 reshape.128
  2.2 0.8 %reshape.118 = bf16[128,32]{1,0:T(8,128)(2,1)S(1)} reshape(bf16[4,1024]{1,0:T(4,128)(2,1)} %param.6) | data formatting | bytes 16384 | tf_op jit(solution)/shard_map/reshape | solution.py:185
  3.0 0.7 %broadcast_multiply_fusion.a_ref = bf16[128,32]{1,0:T(8,128)(2,1)} fusion(bf16[128,32]{1,0:T(8,128)(2,1)S(1)} %reshape.118, bf16[128]{0:T(256)(128)(2,1)S(1)} %reshape.128), kind=kLoop, calls=%fused_computation.3 | loop fusion | flops 4096 | bytes 16640 | tf_op jit(solution)/shard_map/mul | solution.py:185
  3.7 0.8 %reshape.116 = bf16[4,32,32]{2,1,0:T(8,128)(2,1)S(1)} reshape(bf16[4,1024]{1,0:T(4,128)(2,1)} %param.7) | data formatting | bytes 16384 | tf_op jit(solution)/shard_map/reshape | solution.py:186
  4.5 0.1 copy.15
  4.6 0.1 reshape.117
  4.7 0.6 %pad_maximum_fusion.x_ref = bf16[4,1152]{1,0:T(4,128)(2,1)} fusion(bf16[4,128]{1,0:T(4,128)(2,1)S(1)} %broadcast_in_dim.4, bf16[4,1024]{1,0:T(4,128)(2,1)S(1)} %reshape.117), kind=kLoop, calls=%fused_computation.4 | loop fusion | flops 18432 | bytes 18432 | tf_op jit(solution)/shard_map/concatenate | solution.py:187
  5.3 0.1 mul.40
  5.4 0.1 mul.41
  5.5 0.0 copy-done.1
  5.5 0.8 %copy.16 = bf16[32,32,128]{2,0,1:T(8,128)(2,1)} copy(bf16[32,32,128]{2,1,0:T(8,128)(2,1)S(1)} %bitcast.18) | data formatting | bytes 524288 | tf_op jit(solution)/shard_map/reshape | solution.py:188
  6.3 31.3 %shard_map.101 = (bf16[4,64,128]{2,1,0:T(8,128)(2,1)}, f32[128,32]{1,0:T(8,128)}, f32[4,1024]{1,0:T(4,128)}, bf16[16,64,128]{2,1,0:T(8,128)(2,1)}, f32[1,128]{1,0:T(1,128)}) custom-call(bf16[4,1152]{1,0:T(4,128)(2,1)} %pad_maximum_fusion.x_ref, bf16[128,32]{1,0:T(8,128)(2,1)} %broadcast_multiply_fusion.a_ref, bf16[4,64,128]{2,1,0:T(8,128)(2,1)} %cot_ref.1, ...), custom_call_target="tpu_custom_call" | custom-call | tf_op jit(solution)/shard_map/pallas_call | solution.py:190
  37.6 0.0 copy-start.3
  37.6 0.0 copy-start
  37.6 1.0 %reshape.121 = f32[4,1024]{1,0:T(4,128)S(1)} reshape(f32[128,32]{1,0:T(8,128)} %get-tuple-element.11) | data formatting | bytes 32768 | tf_op jit(solution)/shard_map/reshape | solution.py:221
  38.6 0.6 %mul.42 = f32[4,1024]{1,0:T(4,128)} multiply(f32[4,1024]{1,0:T(4,128)S(1)} %reshape.121, f32[4,1024]{1,0:T(4,128)S(1)} %mul.41) | non-fusion elementwise | flops 4096 | bytes 49152 | tf_op jit(solution)/shard_map/mul | solution.py:221
  39.2 0.0 copy-done.3
  39.2 0.1 reshape.122
  39.3 0.1 copy.17
  39.4 0.7 %reshape.123 = f32[4,1024]{1,0:T(4,128)} reshape(f32[4,32,32]{2,1,0:T(8,128)S(1)} %copy.17) | data formatting | bytes 32768 | tf_op jit(solution)/shard_map/reshape | solution.py:222
  40.1 0.0 copy-done
  40.2 0.0 copy-start.2
  40.2 1.1 %copy.18 = f32[32,32,128]{2,1,0:T(8,128)} copy(f32[32,32,128]{2,0,1:T(8,128)S(1)} %convert_bitcast_fusion) | data formatting | bytes 1048576 | tf_op jit(solution)/shard_map/reshape | solution.py:219
  41.3 0.0 copy-done.2
  41.3 0.0 copy-start.4
  41.3 0.6 %copy.21 = bf16[4,64,128]{2,1,0:T(8,128)(2,1)} copy(bf16[4,64,128]{2,1,0:T(8,128)(2,1)S(1)} %copy-done.2) | data formatting | bytes 131072
  41.9 0.1 copy-done.4
  42.0 0.5 %copy.22 = f32[128]{0:T(128)} copy(f32[128]{0:T(128)S(1)} %bitcast.20) | data formatting | bytes 1024
  (3 shorter events, 0.1 us)
Async XLA Ops:
  0.6 4.9 %copy-start.1 = (bf16[1024,128]{1,0:T(8,128)(2,1)S(1)}, bf16[1024,128]{1,0:T(8,128)(2,1)}, u32[]{:S(2)}) copy-start(bf16[1024,128]{1,0:T(8,128)(2,1)} %param.9) | copy-start | bytes 786436
  37.6 1.6 %copy-start.3 = (f32[4,1024]{1,0:T(4,128)S(1)}, f32[4,1024]{1,0:T(4,128)}, u32[]{:S(2)}) copy-start(f32[4,1024]{1,0:T(4,128)} %get-tuple-element.12) | copy-start | bytes 49156
  37.6 2.5 %copy-start = (bf16[16,64,128]{2,1,0:T(8,128)(2,1)S(1)}, bf16[16,64,128]{2,1,0:T(8,128)(2,1)}, u32[]{:S(2)}) copy-start(bf16[16,64,128]{2,1,0:T(8,128)(2,1)} %get-tuple-element.13) | copy-start | bytes 786436
  40.2 1.1 %copy-start.2 = (bf16[4,64,128]{2,1,0:T(8,128)(2,1)S(1)}, bf16[4,64,128]{2,1,0:T(8,128)(2,1)}, u32[]{:S(2)}) copy-start(bf16[4,64,128]{2,1,0:T(8,128)(2,1)} %get-tuple-element.22) | copy-start | bytes 196612
  41.3 0.7 %copy-start.4 = (f32[1,128]{1,0:T(1,128)S(1)}, f32[1,128]{1,0:T(1,128)}, u32[]{:S(2)}) copy-start(f32[1,128]{1,0:T(1,128)} %get-tuple-element.14) | copy-start | bytes 1540

commit v2 on v1

--- a/solution.py
+++ b/solution.py
@@ -31,7 +31,8 @@
 def kernel(
     n, x_ref, a_ref, cot_ref, w_ref, bias_ref,
     pu_ref, gl_ref, gr_ref, gw_ref, gb_ref,
-    gat, bs, uhi, ulo, t_ref, send_w, recv_w, part_r, send_r, recv_r, mine_w, all_w,
+    gat, bs, uhi, ulo, t_ref, pair_w, got_w, send_w, recv_w,
+    part_r, pair_r, got_r, send_r, recv_r, mine_w, all_w,
     send_sems, recv_sems,
 ):
     me = lax.axis_index("pi")
@@ -42,25 +43,73 @@
     total = cot_ref.shape[1]
     chunk = gw_ref.shape[1]
 
-    def copy(k, source, target, peer, slot):
+    core = lax.rem(me, 2)
+    chip = me // 2
+    partner = me + 1 - 2 * core
+    chips = n // 2
+
+    def copy(k, source, target, peer, slot, sent):
         return pltpu.make_async_remote_copy(
-            src_ref=source, dst_ref=target.at[slot],
-            send_sem=send_sems.at[k, peer], recv_sem=recv_sems.at[k, slot],
+            src_ref=source, dst_ref=target,
+            send_sem=send_sems.at[k, sent], recv_sem=recv_sems.at[k, slot],
             device_id={"pi": peer}, device_id_type=MESH,
         )
 
     def each(act):
         def body(step, carry):
-            act(lax.rem(me + step, n))
+            act(lax.rem(me + 2 * step, n))
             return carry
 
-        lax.fori_loop(1, n, body, 0)
+        lax.fori_loop(1, chips, body, 0)
+
+    def other(p):
+        return p + 1 - 2 * core
+
+    def direct(k, source, target, p):
+        return copy(k, source, target.at[me], p, me, p)
+
+    def landed(k, target, p):
+        return copy(k, target.at[p], target.at[p], partner, p, other(p))
+
+    def gather_start(k, source, target):
+        each(lambda p: direct(k, source, target, p).start())
+        direct(k, source, target, partner).start()
+        target[me] = source[...]
+
+    def gather_pass(k, target):
+        def act(p):
+            landed(k, target, p).wait_recv()
+            landed(k, target, p).start()
+
+        each(act)
+
+    def gather_end(k, target):
+        landed(k, target, partner).wait_recv()
+        each(lambda p: landed(k, target, other(p)).wait_recv())
+
+    def gather_sent(k, source, target):
+        each(lambda p: direct(k, source, target, p).wait_send())
+        direct(k, source, target, partner).wait_send()
+        each(lambda p: landed(k, target, p).wait_send())
+
+    def pair(index, source, target):
+        return copy(4, source.at[1 - core], target, partner, index, index)
+
+    def across(k, source, target, p):
+        return copy(k, source.at[p // 2], target.at[chip], p, me, p)
+
+    def across_in(k, source, target, p):
+        return copy(k, source.at[p // 2], target.at[p // 2], p, p, p)
 
     barrier = pltpu.get_barrier_semaphore()
-    each(lambda p: pl.semaphore_signal(barrier, inc=1, device_id={"pi": p}, device_id_type=MESH))
-    pl.semaphore_wait(barrier, n - 1)
-    each(lambda p: copy(0, x_ref, gat, p, me).start())
-    gat[me] = x_ref[...]
+
+    def greet(p):
+        pl.semaphore_signal(barrier, inc=1, device_id={"pi": p}, device_id_type=MESH)
+
+    each(greet)
+    greet(partner)
+    pl.semaphore_wait(barrier, chips)
+    gather_start(0, x_ref, gat)
 
     a = a_ref[...]
     for d in range(C):
@@ -71,7 +120,8 @@
             ulo[here] = low[i * samples:(i + 1) * samples]
     a_t = jnp.concatenate([a, a], axis=0).astype(F32).T.astype(BF16)
 
-    each(lambda p: copy(0, x_ref, gat, p, p).wait_recv())
+    gather_pass(0, gat)
+    gather_end(0, gat)
 
     def gather_rows(q, carry):
         both = jnp.concatenate([gat[2 * q].astype(F32), gat[2 * q + 1].astype(F32)], axis=0)
@@ -101,55 +151,78 @@
             [t_ref[d * samples:(d + 1) * samples, i * z:(i + 1) * z] for i in range(rows)], axis=0
         )
 
-    sum_high, sum_low = split(cot_sum)
     per = max(1, chunk // C)
     for d in range(C):
         high, low = split(t_of(d))
-        piece = mm(a_t, jnp.concatenate([high, low], axis=0)).astype(BF16)
+        piece = mm(a_t, jnp.concatenate([high, low], axis=0))
         if chunk >= C:
-            send_w[d // per, (d % per) * C:(d % per + 1) * C, :] = piece
+            p = d // per
+            pair_w[p % 2, p // 2, (d % per) * C:(d % per + 1) * C, :] = piece
         else:
             for k in range(C // chunk):
-                send_w[d * (C // chunk) + k, :chunk, :] = piece[k * chunk:(k + 1) * chunk]
-    sums = jnp.concatenate(
-        [sum_high.astype(F32), sum_low.astype(F32), jnp.zeros((EXTRA - 2, z), F32)], axis=0
-    ).astype(BF16)
-
-    def put_sums(p, carry):
-        send_w[p, chunk:, :] = sums
-        return carry
-
-    lax.fori_loop(0, n, put_sums, 0)
-    each(lambda p: copy(1, send_w.at[p], recv_w, p, me).start())
-    recv_w[me] = send_w[me]
+                p = d * (C // chunk) + k
+                pair_w[p % 2, p // 2, :chunk, :] = piece[k * chunk:(k + 1) * chunk]
+    sums = jnp.concatenate([cot_sum, jnp.zeros((EXTRA - 1, z), F32)], axis=0)
+
+    def put_sums(m, carry):
+        pair_w[0, m, chunk:, :] = sums
+        pair_w[1, m, chunk:, :] = sums
+        return carry
+
+    lax.fori_loop(0, chips, put_sums, 0)
+    pair(0, pair_w, got_w).start()
 
     u_high = uhi[...]
     part_r[...] = mm_nt(cot_high, u_high) + mm_nt(cot_low, u_high) + mm_nt(cot_high, ulo[...])
 
     def scatter_rows(q, carry):
         both = part_r[pl.ds(pl.multiple_of(q * 2 * rows, 2 * rows), 2 * rows), :]
-        send_r[2 * q] = both[:rows].astype(BF16)
-        send_r[2 * q + 1] = both[rows:].astype(BF16)
-        return carry
-
-    lax.fori_loop(0, n // 2, scatter_rows, 0)
-    each(lambda p: copy(2, send_r.at[p], recv_r, p, me).start())
-    recv_r[me] = send_r[me]
-
-    each(lambda p: copy(1, send_w.at[p], recv_w, p, p).wait_recv())
-
-    def add_w(p, acc):
-        return acc + recv_w[p].astype(F32)
-
-    total_w = lax.fori_loop(0, n, add_w, jnp.zeros((chunk + EXTRA, z), F32))
-    mine_w[...] = total_w[:chunk].astype(BF16)
-    gb_ref[...] = total_w[chunk:chunk + 1] + total_w[chunk + 1:chunk + 2]
-    each(lambda p: copy(3, mine_w, all_w, p, me).start())
-    all_w[me] = mine_w[...]
+        pair_r[0, q] = both[:rows]
+        pair_r[1, q] = both[rows:]
+        return carry
+
+    lax.fori_loop(0, chips, scatter_rows, 0)
+    pair(1, pair_r, got_r).start()
+
+    pair(0, pair_w, got_w).wait_recv()
+
+    def join_w(m, carry):
+        both = pair_w[core, m] + got_w[m]
+        high, low = split(both[chunk:chunk + 1])
+        tail = jnp.concatenate(
+            [high.astype(F32), low.astype(F32), jnp.zeros((EXTRA - 2, z), F32)], axis=0
+        )
+        send_w[m, :chunk, :] = both[:chunk].astype(BF16)
+        send_w[m, chunk:, :] = tail.astype(BF16)
+        return carry
+
+    lax.fori_loop(0, chips, join_w, 0)
+    each(lambda p: across(1, send_w, recv_w, p).start())
+    recv_w[chip] = send_w[chip]
+
+    pair(1, pair_r, got_r).wait_recv()
+
+    def join_r(m, carry):
+        send_r[m] = (pair_r[core, m] + got_r[m]).astype(BF16)
+        return carry
+
+    lax.fori_loop(0, chips, join_r, 0)
+    each(lambda p: across(2, send_r, recv_r, p).start())
+    recv_r[chip] = send_r[chip]
 
     update = mm(b, u_high) + mm(b, ulo[...])
     for i in range(rows):
         pu_ref[i] = (update[:, i * z:(i + 1) * z] * inverse[i] + bias_ref[...]).astype(BF16)
+
+    each(lambda p: across_in(1, send_w, recv_w, p).wait_recv())
+
+    def add_w(m, acc):
+        return acc + recv_w[m].astype(F32)
+
+    total_w = lax.fori_loop(0, chips, add_w, jnp.zeros((chunk + EXTRA, z), F32))
+    mine_w[...] = total_w[:chunk].astype(BF16)
+    gb_ref[...] = total_w[chunk:chunk + 1] + total_w[chunk + 1:chunk + 2]
+    gather_start(3, mine_w, all_w)
 
     left_acc = jnp.zeros((rows * samples, C), F32)
     for d in range(C):
@@ -160,19 +233,22 @@
         )
     gl_ref[...] = left_acc
 
-    each(lambda p: copy(2, send_r.at[p], recv_r, p, p).wait_recv())
-
-    def add_r(p, acc):
-        return acc + recv_r[p].astype(F32)
-
-    gr_ref[...] = lax.fori_loop(0, n, add_r, jnp.zeros((rows, width), F32))
-
-    each(lambda p: copy(3, mine_w, all_w, p, p).wait_recv())
+    gather_pass(3, all_w)
+    each(lambda p: across_in(2, send_r, recv_r, p).wait_recv())
+
+    def add_r(m, acc):
+        return acc + recv_r[m].astype(F32)
+
+    gr_ref[...] = lax.fori_loop(0, chips, add_r, jnp.zeros((rows, width), F32))
+
+    gather_end(3, all_w)
     gw_ref[...] = all_w[...]
-    each(lambda p: copy(0, x_ref, gat, p, me).wait_send())
-    each(lambda p: copy(1, send_w.at[p], recv_w, p, me).wait_send())
-    each(lambda p: copy(2, send_r.at[p], recv_r, p, me).wait_send())
-    each(lambda p: copy(3, mine_w, all_w, p, me).wait_send())
+    gather_sent(0, x_ref, gat)
+    gather_sent(3, mine_w, all_w)
+    pair(0, pair_w, got_w).wait_send()
+    pair(1, pair_r, got_r).wait_send()
+    each(lambda p: across(1, send_w, recv_w, p).wait_send())
+    each(lambda p: across(2, send_r, recv_r, p).wait_send())
 
 
 def local(n, left, right, depth, w_out, bias, pair_cot):
@@ -204,15 +280,19 @@
             pltpu.VMEM((C * samples, rows * z), BF16),
             pltpu.VMEM((C * samples, rows * z), BF16),
             pltpu.VMEM((C * samples, rows * z), F32),
-            pltpu.VMEM((n, chunk + EXTRA, z), BF16),
-            pltpu.VMEM((n, chunk + EXTRA, z), BF16),
+            pltpu.VMEM((2, n // 2, chunk + EXTRA, z), F32),
+            pltpu.VMEM((n // 2, chunk + EXTRA, z), F32),
+            pltpu.VMEM((n // 2, chunk + EXTRA, z), BF16),
+            pltpu.VMEM((n // 2, chunk + EXTRA, z), BF16),
             pltpu.VMEM((total, width), F32),
-            pltpu.VMEM((n, rows, width), BF16),
-            pltpu.VMEM((n, rows, width), BF16),
+            pltpu.VMEM((2, n // 2, rows, width), F32),
+            pltpu.VMEM((n // 2, rows, width), F32),
+            pltpu.VMEM((n // 2, rows, width), BF16),
+            pltpu.VMEM((n // 2, rows, width), BF16),
             pltpu.VMEM((chunk, z), BF16),
             pltpu.VMEM((n, chunk, z), BF16),
-            pltpu.SemaphoreType.DMA((4, n)),
-            pltpu.SemaphoreType.DMA((4, n)),
+            pltpu.SemaphoreType.DMA((5, n)),
+            pltpu.SemaphoreType.DMA((5, n)),
         ],
         compiler_params=pltpu.CompilerParams(collective_id=0, has_side_effects=True),
     )(x, a, pair_cot, w, bias[None, :])

time: 42.8 us -> 39.8 us (0.930)
  Pallas kernels: 31.3 us -> 28.3 us
    pallas_call x1, Pallas kernels: 31.3 us -> 28.3 us  [local(): pl.pallas_call(functools.partial(kernel, n), out_shape=(jax.ShapeDtypeStr...]
where the time goes in v2:
time: 39.8 us; the launch traced here: 39.6 us
  Pallas kernels  28.3 us (71%)
  local copies, waits for them, and re-layouts  7.07 us (18%)
  other arithmetic  3.42 us (9%)
  between operations  0.73 us (2%)
    pallas_call x1, Pallas kernels, local(): pl.pallas_call(functools.partial(kernel, n), out_shape=(jax.ShapeDtypeStr...  28.3 us
    unnamed x12, local copies, waits for them, and re-layouts  1.21 us
    reshape x1, local copies, waits for them, and re-layouts, local(): gw.astype(F32).reshape(C, C, z).transpose(1, 0, 2).reshape(C * C, z)  1.1 us
    reshape x1, local copies, waits for them, and re-layouts, local(): gl.reshape(rows, samples, C) * keep[:, :, None]  0.98 us
    reshape x2, local copies, waits for them, and re-layouts, local(): right.reshape(rows, samples, C) * own  0.88 us
    reshape x1, local copies, waits for them, and re-layouts, local(): w = w_out.reshape(C, C, z).transpose(1, 0, 2).reshape(C * C, z)  0.81 us

profile of v2, /device:TPU:1, one launch (start us, length us, event | category | flops | bytes accessed | tf_op | source)
XLA Modules:
  0.0 39.6 jit_solution(9684250474235492201)
XLA Ops:
  0.6 0.0 copy-start.1
  0.6 0.7 %convert_element_type.29 = bf16[4]{0:T(256)(128)(2,1)S(1)} convert(s32[4]{0:T(128)} %param.8) | non-fusion elementwise | flops 4 | bytes 24 | tf_op jit(solution)/shard_map/convert_element_type | solution.py:263
  1.3 0.1 broadcast_in_dim.4
  1.4 0.7 %fusion = (f32[4,32]{1,0:T(4,128)S(1)}, bf16[4,32]{1,0:T(4,128)(2,1)S(1)}) fusion(s32[4]{0:T(128)} %param.8), kind=kLoop, calls=%fused_computation.6 | loop fusion | flops 384 | bytes 784 | tf_op jit(solution)/shard_map/convert_element_type | solution.py:300
  2.1 0.1 reshape.128
  2.2 0.8 %reshape.118 = bf16[128,32]{1,0:T(8,128)(2,1)S(1)} reshape(bf16[4,1024]{1,0:T(4,128)(2,1)} %param.6) | data formatting | bytes 16384 | tf_op jit(solution)/shard_map/reshape | solution.py:261
  3.0 0.7 %broadcast_multiply_fusion.a_ref = bf16[128,32]{1,0:T(8,128)(2,1)} fusion(bf16[128,32]{1,0:T(8,128)(2,1)S(1)} %reshape.118, bf16[128]{0:T(256)(128)(2,1)S(1)} %reshape.128), kind=kLoop, calls=%fused_computation.3 | loop fusion | flops 4096 | bytes 16640 | tf_op jit(solution)/shard_map/mul | solution.py:261
  3.7 0.8 %reshape.116 = bf16[4,32,32]{2,1,0:T(8,128)(2,1)S(1)} reshape(bf16[4,1024]{1,0:T(4,128)(2,1)} %param.7) | data formatting | bytes 16384 | tf_op jit(solution)/shard_map/reshape | solution.py:262
  4.5 0.1 copy.15
  4.6 0.1 reshape.117
  4.7 0.6 %pad_maximum_fusion.x_ref = bf16[4,1152]{1,0:T(4,128)(2,1)} fusion(bf16[4,128]{1,0:T(4,128)(2,1)S(1)} %broadcast_in_dim.4, bf16[4,1024]{1,0:T(4,128)(2,1)S(1)} %reshape.117), kind=kLoop, calls=%fused_computation.4 | loop fusion | flops 18432 | bytes 18432 | tf_op jit(solution)/shard_map/concatenate | solution.py:263
  5.3 0.1 mul.40
  5.4 0.1 mul.41
  5.5 0.0 copy-done.1
  5.5 0.8 %copy.16 = bf16[32,32,128]{2,0,1:T(8,128)(2,1)} copy(bf16[32,32,128]{2,1,0:T(8,128)(2,1)S(1)} %bitcast.18) | data formatting | bytes 524288 | tf_op jit(solution)/shard_map/reshape | solution.py:264
  6.3 28.3 %shard_map.101 = (bf16[4,64,128]{2,1,0:T(8,128)(2,1)}, f32[128,32]{1,0:T(8,128)}, f32[4,1024]{1,0:T(4,128)}, bf16[16,64,128]{2,1,0:T(8,128)(2,1)}, f32[1,128]{1,0:T(1,128)}) custom-call(bf16[4,1152]{1,0:T(4,128)(2,1)} %pad_maximum_fusion.x_ref, bf16[128,32]{1,0:T(8,128)(2,1)} %broadcast_multiply_fusion.a_ref, bf16[4,64,128]{2,1,0:T(8,128)(2,1)} %cot_ref.1, ...), custom_call_target="tpu_custom_call" | custom-call | tf_op jit(solution)/shard_map/pallas_call | solution.py:266
  34.7 0.0 copy-start.3
  34.7 0.0 copy-start
  34.7 1.0 %reshape.121 = f32[4,1024]{1,0:T(4,128)S(1)} reshape(f32[128,32]{1,0:T(8,128)} %get-tuple-element.11) | data formatting | bytes 32768 | tf_op jit(solution)/shard_map/reshape | solution.py:301
  35.7 0.6 %mul.42 = f32[4,1024]{1,0:T(4,128)} multiply(f32[4,1024]{1,0:T(4,128)S(1)} %reshape.121, f32[4,1024]{1,0:T(4,128)S(1)} %mul.41) | non-fusion elementwise | flops 4096 | bytes 49152 | tf_op jit(solution)/shard_map/mul | solution.py:301
  36.3 0.0 copy-done.3
  36.3 0.1 reshape.122
  36.4 0.1 copy.17
  36.5 0.7 %reshape.123 = f32[4,1024]{1,0:T(4,128)} reshape(f32[4,32,32]{2,1,0:T(8,128)S(1)} %copy.17) | data formatting | bytes 32768 | tf_op jit(solution)/shard_map/reshape | solution.py:302
  37.2 0.0 copy-done
  37.2 0.0 copy-start.2
  37.3 1.1 %copy.18 = f32[32,32,128]{2,1,0:T(8,128)} copy(f32[32,32,128]{2,0,1:T(8,128)S(1)} %convert_bitcast_fusion) | data formatting | bytes 1048576 | tf_op jit(solution)/shard_map/reshape | solution.py:299
  38.4 0.0 copy-done.2
  38.4 0.0 copy-start.4
  38.4 0.6 %copy.21 = bf16[4,64,128]{2,1,0:T(8,128)(2,1)} copy(bf16[4,64,128]{2,1,0:T(8,128)(2,1)S(1)} %copy-done.2) | data formatting | bytes 131072
  39.0 0.1 copy-done.4
  39.0 0.5 %copy.22 = f32[128]{0:T(128)} copy(f32[128]{0:T(128)S(1)} %bitcast.20) | data formatting | bytes 1024
  (3 shorter events, 0.1 us)
Async XLA Ops:
  0.6 4.9 %copy-start.1 = (bf16[1024,128]{1,0:T(8,128)(2,1)S(1)}, bf16[1024,128]{1,0:T(8,128)(2,1)}, u32[]{:S(2)}) copy-start(bf16[1024,128]{1,0:T(8,128)(2,1)} %param.9) | copy-start | bytes 786436
  34.7 1.6 %copy-start.3 = (f32[4,1024]{1,0:T(4,128)S(1)}, f32[4,1024]{1,0:T(4,128)}, u32[]{:S(2)}) copy-start(f32[4,1024]{1,0:T(4,128)} %get-tuple-element.12) | copy-start | bytes 49156
  34.7 2.5 %copy-start = (bf16[16,64,128]{2,1,0:T(8,128)(2,1)S(1)}, bf16[16,64,128]{2,1,0:T(8,128)(2,1)}, u32[]{:S(2)}) copy-start(bf16[16,64,128]{2,1,0:T(8,128)(2,1)} %get-tuple-element.13) | copy-start | bytes 786436
  37.2 1.1 %copy-start.2 = (bf16[4,64,128]{2,1,0:T(8,128)(2,1)S(1)}, bf16[4,64,128]{2,1,0:T(8,128)(2,1)}, u32[]{:S(2)}) copy-start(bf16[4,64,128]{2,1,0:T(8,128)(2,1)} %get-tuple-element.22) | copy-start | bytes 196612
  38.4 0.7 %copy-start.4 = (f32[1,128]{1,0:T(1,128)S(1)}, f32[1,128]{1,0:T(1,128)}, u32[]{:S(2)}) copy-start(f32[1,128]{1,0:T(1,128)} %get-tuple-element.14) | copy-start | bytes 1540

commit v3 on v2

--- a/solution.py
+++ b/solution.py
@@ -29,16 +29,15 @@
 
 
 def kernel(
-    n, x_ref, a_ref, cot_ref, w_ref, bias_ref,
+    n, left_ref, right_ref, depth_ref, cot_ref, w_in, bias_ref,
     pu_ref, gl_ref, gr_ref, gw_ref, gb_ref,
-    gat, bs, uhi, ulo, t_ref, pair_w, got_w, send_w, recv_w,
+    x_ref, w_ref, u_ref, gw_part, gat, bs, uhi, ulo, t_ref, pair_w, got_w, send_w, recv_w,
     part_r, pair_r, got_r, send_r, recv_r, mine_w, all_w,
     send_sems, recv_sems,
 ):
     me = lax.axis_index("pi")
-    rows = x_ref.shape[0]
-    z = w_ref.shape[1]
-    width = x_ref.shape[1] - z
+    rows, width = right_ref.shape
+    z = w_in.shape[1]
     samples = width // C
     total = cot_ref.shape[1]
     chunk = gw_ref.shape[1]
@@ -108,17 +107,56 @@
 
     each(greet)
     greet(partner)
+    spot = (rows, rows)
+    wide = jnp.broadcast_to(depth_ref[...], spot).astype(F32)
+    diagonal = lax.broadcasted_iota(jnp.int32, spot, 0) == lax.broadcasted_iota(jnp.int32, spot, 1)
+    own_depth = jnp.sum(jnp.where(diagonal, wide, 0.0), axis=1, keepdims=True)
+    x_ref[:, :width] = right_ref[...]
+    x_ref[:, width:] = jnp.broadcast_to(own_depth, (rows, z)).astype(BF16)
     pl.semaphore_wait(barrier, chips)
     gather_start(0, x_ref, gat)
 
-    a = a_ref[...]
+    def sample_of(count):
+        return lax.broadcasted_iota(jnp.int32, (count, width), 1) // C
+
+    def kept(count, depths):
+        return sample_of(count).astype(F32) < depths
+
+    line = lax.broadcasted_iota(jnp.int32, (samples, width), 0)
+    diagonal = sample_of(samples) == line
+    own_lines = [
+        diagonal & (line.astype(F32) < jnp.broadcast_to(own_depth[i:i + 1], (samples, width)))
+        for i in range(rows)
+    ]
+    fold = (
+        lax.broadcasted_iota(jnp.int32, (width, C), 0) % C
+        == lax.broadcasted_iota(jnp.int32, (width, C), 1)
+    ).astype(F32).astype(BF16)
+    unfold = (
+        lax.broadcasted_iota(jnp.int32, (C, width), 1) % C
+        == lax.broadcasted_iota(jnp.int32, (C, width), 0)
+    ).astype(F32).astype(BF16)
+    left = left_ref[...].astype(F32)
+    spread = [
+        jnp.where(own_lines[i], jnp.broadcast_to(left[i:i + 1], (samples, width)), 0.0)
+        for i in range(rows)
+    ]
+    a32 = mm(jnp.concatenate(spread, axis=0).astype(BF16), fold)
+    a = a32.astype(BF16)
+    w_ref[...] = w_in[...].astype(F32)
+
+    def w_of(d):
+        return w_ref[pl.ds(d, C, stride=C), :].astype(BF16)
+
     for d in range(C):
-        high, low = split(mm(a, w_ref[d * C:(d + 1) * C, :]))
+        product = mm(a, w_of(d))
         for i in range(rows):
-            here = (slice(d * samples, (d + 1) * samples), slice(i * z, (i + 1) * z))
-            uhi[here] = high[i * samples:(i + 1) * samples]
-            ulo[here] = low[i * samples:(i + 1) * samples]
-    a_t = jnp.concatenate([a, a], axis=0).astype(F32).T.astype(BF16)
+            u_ref[pl.ds(i * width + d, samples, stride=C), :] = product[i * samples:(i + 1) * samples]
+    for i in range(rows):
+        high, low = split(u_ref[i * width:(i + 1) * width])
+        uhi[:, i * z:(i + 1) * z] = high
+        ulo[:, i * z:(i + 1) * z] = low
+    a_t = jnp.concatenate([a32, a32], axis=0).T.astype(BF16)
 
     gather_pass(0, gat)
     gather_end(0, gat)
@@ -129,13 +167,15 @@
         return carry
 
     lax.fori_loop(0, n // 2, gather_rows, 0)
-    b32 = bs[:, :width]
+    depths = bs[:, width:]
+    b32 = jnp.where(
+        kept(total, jnp.concatenate([depths] * (width // z), axis=1)), bs[:, :width], 0.0
+    )
     b = b32.astype(BF16)
-    depths = bs[:, width:]
     inverse, highs, lows = [], [], []
     cot_sum = jnp.zeros((1, z), F32)
     for i in range(rows):
-        inverse.append(1.0 / (EPSILON + jnp.minimum(depths, x_ref[i:i + 1, width:].astype(F32))))
+        inverse.append(1.0 / (EPSILON + jnp.minimum(depths, own_depth[i:i + 1])))
         cot = cot_ref[i].astype(F32)
         cot_sum = cot_sum + jnp.sum(cot, axis=0, keepdims=True)
         high, low = split(cot * inverse[i])
@@ -144,24 +184,20 @@
     cot_high = jnp.concatenate(highs, axis=1)
     cot_low = jnp.concatenate(lows, axis=1)
     b_t = jnp.concatenate([b32, b32], axis=0).T.astype(BF16)
-    t_ref[...] = mm(b_t, jnp.concatenate([cot_high, cot_low], axis=0))
+    t = mm(b_t, jnp.concatenate([cot_high, cot_low], axis=0))
+    for i in range(rows):
+        t_ref[i * width:(i + 1) * width, :] = t[:, i * z:(i + 1) * z]
 
     def t_of(d):
         return jnp.concatenate(
-            [t_ref[d * samples:(d + 1) * samples, i * z:(i + 1) * z] for i in range(rows)], axis=0
-        )
-
-    per = max(1, chunk // C)
+            [t_ref[pl.ds(i * width + d, samples, stride=C), :] for i in range(rows)], axis=0
+        )
+
     for d in range(C):
         high, low = split(t_of(d))
-        piece = mm(a_t, jnp.concatenate([high, low], axis=0))
-        if chunk >= C:
-            p = d // per
-            pair_w[p % 2, p // 2, (d % per) * C:(d % per + 1) * C, :] = piece
-        else:
-            for k in range(C // chunk):
-                p = d * (C // chunk) + k
-                pair_w[p % 2, p // 2, :chunk, :] = piece[k * chunk:(k + 1) * chunk]
+        gw_part[pl.ds(d, C, stride=C), :] = mm(a_t, jnp.concatenate([high, low], axis=0))
+    for p in range(n):
+        pair_w[p % 2, p // 2, :chunk, :] = gw_part[p * chunk:(p + 1) * chunk]
     sums = jnp.concatenate([cot_sum, jnp.zeros((EXTRA - 1, z), F32)], axis=0)
 
     def put_sums(m, carry):
@@ -227,11 +263,16 @@
     left_acc = jnp.zeros((rows * samples, C), F32)
     for d in range(C):
         high, low = split(t_of(d))
-        w_d = w_ref[d * C:(d + 1) * C, :]
+        w_d = w_of(d)
         left_acc = left_acc + mm_nt(
             jnp.concatenate([high, low], axis=1), jnp.concatenate([w_d, w_d], axis=1)
         )
-    gl_ref[...] = left_acc
+    high, low = split(left_acc)
+    lines = mm(high, unfold) + mm(low, unfold)
+    for i in range(rows):
+        gl_ref[i:i + 1, :] = jnp.sum(
+            jnp.where(own_lines[i], lines[i * samples:(i + 1) * samples], 0.0), axis=0, keepdims=True
+        )
 
     gather_pass(3, all_w)
     each(lambda p: across_in(2, send_r, recv_r, p).wait_recv())
@@ -239,10 +280,11 @@
     def add_r(m, acc):
         return acc + recv_r[m].astype(F32)
 
-    gr_ref[...] = lax.fori_loop(0, chips, add_r, jnp.zeros((rows, width), F32))
+    total_r = lax.fori_loop(0, chips, add_r, jnp.zeros((rows, width), F32))
+    gr_ref[...] = jnp.where(kept(rows, jnp.broadcast_to(own_depth, (rows, width))), total_r, 0.0)
 
     gather_end(3, all_w)
-    gw_ref[...] = all_w[...]
+    gw_ref[...] = all_w[...].astype(F32)
     gather_sent(0, x_ref, gat)
     gather_sent(3, mine_w, all_w)
     pair(0, pair_w, got_w).wait_send()
@@ -253,33 +295,30 @@
 
 def local(n, left, right, depth, w_out, bias, pair_cot):
     rows, width = left.shape
-    samples = width // C
     total, z = pair_cot.shape[1:]
     chunk = w_out.shape[0] // n
-    mask = jnp.arange(samples, dtype=jnp.int32)[None, :] < depth[:, None]
-    own = mask.astype(BF16)[:, :, None]
-    a = (left.reshape(rows, samples, C) * own).reshape(rows * samples, C)
-    b = (right.reshape(rows, samples, C) * own).transpose(0, 2, 1).reshape(rows, width)
-    x = jnp.concatenate([b, jnp.broadcast_to(depth.astype(BF16)[:, None], (rows, z))], axis=1)
-    w = w_out.reshape(C, C, z).transpose(1, 0, 2).reshape(C * C, z)
     vmem = pl.BlockSpec(memory_space=pltpu.VMEM)
     pu, gl, gr, gw, gb = pl.pallas_call(
         functools.partial(kernel, n),
         out_shape=(
             jax.ShapeDtypeStruct((rows, total, z), BF16),
-            jax.ShapeDtypeStruct((rows * samples, C), F32),
             jax.ShapeDtypeStruct((rows, width), F32),
-            jax.ShapeDtypeStruct((n, chunk, z), BF16),
+            jax.ShapeDtypeStruct((rows, width), F32),
+            jax.ShapeDtypeStruct((n, chunk, z), F32),
             jax.ShapeDtypeStruct((1, z), F32),
         ),
-        in_specs=[vmem] * 5,
+        in_specs=[vmem] * 6,
         out_specs=(vmem,) * 5,
         scratch_shapes=[
+            pltpu.VMEM((rows, width + z), BF16),
+            pltpu.VMEM((C * C, z), F32),
+            pltpu.VMEM((rows * width, z), F32),
+            pltpu.VMEM((C * C, z), F32),
             pltpu.VMEM((n, rows, width + z), BF16),
             pltpu.VMEM((total, width + z), F32),
-            pltpu.VMEM((C * samples, rows * z), BF16),
-            pltpu.VMEM((C * samples, rows * z), BF16),
-            pltpu.VMEM((C * samples, rows * z), F32),
+            pltpu.VMEM((width, rows * z), BF16),
+            pltpu.VMEM((width, rows * z), BF16),
+            pltpu.VMEM((rows * width, z), F32),
             pltpu.VMEM((2, n // 2, chunk + EXTRA, z), F32),
             pltpu.VMEM((n // 2, chunk + EXTRA, z), F32),
             pltpu.VMEM((n // 2, chunk + EXTRA, z), BF16),
@@ -295,12 +334,8 @@
             pltpu.SemaphoreType.DMA((5, n)),
         ],
         compiler_params=pltpu.CompilerParams(collective_id=0, has_side_effects=True),
-    )(x, a, pair_cot, w, bias[None, :])
-    grad_w = gw.astype(F32).reshape(C, C, z).transpose(1, 0, 2).reshape(C * C, z)
-    keep = mask.astype(F32)
-    grad_left = (gl.reshape(rows, samples, C) * keep[:, :, None]).reshape(rows, width)
-    grad_right = (gr.reshape(rows, C, samples) * keep[:, None, :]).transpose(0, 2, 1).reshape(rows, width)
-    return pu, grad_left, grad_right, grad_w, gb.reshape(z)
+    )(left, right, depth[None, :], pair_cot, w_out, bias[None, :])
+    return pu, gl, gr, gw.reshape(C * C, z), gb.reshape(z)
 
 
 def solution(mesh):

time: 39.8 us -> 35.8 us (0.90)
  other arithmetic: 3.42 us -> 0 us
  local copies, waits for them, and re-layouts: 7.07 us -> 5.2 us
  Pallas kernels: 28.3 us -> 29.6 us
    reshape x9 -> x0, local copies, waits for them, and re-layouts: 5.45 us -> none  [the longest x1 1.1 us: local(): gw.astype(F32).reshape(C, C, z).transpose(1, 0, 2).reshape(C * C, z)]
    unnamed x12 -> x11, local copies, waits for them, and re-layouts: 1.21 us -> 5.2 us
    convert_element_type x2 -> x0, other arithmetic: 1.43 us -> none  [the longest x1 0.73 us: local(): keep = mask.astype(F32)]
    mul x2 -> x0, other arithmetic: 1.31 us -> none  [the longest x1 0.7 us: local(): a = (left.reshape(rows, samples, C) * own).reshape(rows * samples, C)]
    pallas_call x1, Pallas kernels: 28.3 us -> 29.6 us  [local(): pl.pallas_call(functools.partial(kernel, n), out_shape=(jax.ShapeDtypeStr...]
    concatenate x1 -> x0, other arithmetic: 0.61 us -> none  [local(): jnp.concatenate([b, jnp.broadcast_to(depth.astype(BF16)[:, None], (rows,...]
where the time goes in v3:
time: 35.8 us; the launch traced here: 35.5 us
  Pallas kernels  29.6 us (83%)
  local copies, waits for them, and re-layouts  5.2 us (15%)
  between operations  0.65 us (2%)
    pallas_call x1, Pallas kernels, local(): pl.pallas_call(functools.partial(kernel, n), out_shape=(jax.ShapeDtypeStr...  29.6 us
    unnamed x11, local copies, waits for them, and re-layouts  5.2 us

profile of v3, /device:TPU:1, one launch (start us, length us, event | category | flops | bytes accessed | tf_op | source)
XLA Modules:
  0.0 35.5 jit_solution(16312414827772665059)
XLA Ops:
  0.6 29.6 %shard_map.101 = (bf16[4,64,128]{2,1,0:T(8,128)(2,1)}, f32[4,1024]{1,0:T(4,128)}, f32[4,1024]{1,0:T(4,128)}, f32[16,64,128]{2,1,0:T(8,128)}, f32[1,128]{1,0:T(1,128)}) custom-call(bf16[4,1024]{1,0:T(4,128)(2,1)} %left_ref.1, bf16[4,1024]{1,0:T(4,128)(2,1)} %right_ref.1, s32[1,4]{1,0:T(1,128)} %bitcast.5, bf16[4,64,128]{2,1,0:T(8,128)(2,1)} %cot_ref.1, ...), custom_call_target="tpu_custom_call" | custom-call | tf_op jit(solution)/shard_map/pallas_call | solution.py:301
  30.3 0.0 copy-start.1
  30.3 1.5 %copy.16 = bf16[4,64,128]{2,1,0:T(8,128)(2,1)} copy(bf16[4,64,128]{2,1,0:T(8,128)(2,1)} %get-tuple-element.20) | data formatting | bytes 131072
  31.8 0.0 copy-done.1
  31.8 0.0 copy-start
  31.8 0.6 %copy.17 = f32[4,1024]{1,0:T(4,128)} copy(f32[4,1024]{1,0:T(4,128)S(1)} %copy-done.1) | data formatting | bytes 32768
  32.4 0.1 copy-done
  32.5 0.6 %copy.18 = f32[4,1024]{1,0:T(4,128)} copy(f32[4,1024]{1,0:T(4,128)S(1)} %copy-done) | data formatting | bytes 32768
  33.1 0.0 copy-start.2
  33.1 1.9 %copy.19 = f32[1024,128]{1,0:T(8,128)} copy(f32[1024,128]{1,0:T(8,128)} %bitcast.4) | data formatting | bytes 1048576
  35.0 0.0 copy-done.2
  35.0 0.5 %copy.20 = f32[128]{0:T(128)} copy(f32[128]{0:T(128)S(1)} %bitcast.7) | data formatting | bytes 1024
Async XLA Ops:
  30.3 1.5 %copy-start.1 = (f32[4,1024]{1,0:T(4,128)S(1)}, f32[4,1024]{1,0:T(4,128)}, u32[]{:S(2)}) copy-start(f32[4,1024]{1,0:T(4,128)} %get-tuple-element.21) | copy-start | bytes 49156
  31.8 0.7 %copy-start = (f32[4,1024]{1,0:T(4,128)S(1)}, f32[4,1024]{1,0:T(4,128)}, u32[]{:S(2)}) copy-start(f32[4,1024]{1,0:T(4,128)} %get-tuple-element.22) | copy-start | bytes 49156
  33.1 1.9 %copy-start.2 = (f32[1,128]{1,0:T(1,128)S(1)}, f32[1,128]{1,0:T(1,128)}, u32[]{:S(2)}) copy-start(f32[1,128]{1,0:T(1,128)} %get-tuple-element.14) | copy-start | bytes 1540

commit v4 on v3

--- a/solution.py
+++ b/solution.py
@@ -9,7 +9,6 @@
 
 C = 32
 EPSILON = 0.001
-EXTRA = 16
 MESH = pl.DeviceIdType.MESH
 F32 = jnp.float32
 BF16 = jnp.bfloat16
@@ -112,7 +111,14 @@
     diagonal = lax.broadcasted_iota(jnp.int32, spot, 0) == lax.broadcasted_iota(jnp.int32, spot, 1)
     own_depth = jnp.sum(jnp.where(diagonal, wide, 0.0), axis=1, keepdims=True)
     x_ref[:, :width] = right_ref[...]
-    x_ref[:, width:] = jnp.broadcast_to(own_depth, (rows, z)).astype(BF16)
+    x_ref[:, width:width + z] = jnp.broadcast_to(own_depth, (rows, z)).astype(BF16)
+    cot_sum = jnp.zeros((1, z), F32)
+    for i in range(rows):
+        cot_sum = cot_sum + jnp.sum(cot_ref[i].astype(F32), axis=0, keepdims=True)
+    high, low = split(cot_sum)
+    x_ref[:, width + z:] = jnp.concatenate(
+        [high.astype(F32), low.astype(F32), jnp.zeros((rows - 2, z), F32)], axis=0
+    ).astype(BF16)
     pl.semaphore_wait(barrier, chips)
     gather_start(0, x_ref, gat)
 
@@ -167,17 +173,16 @@
         return carry
 
     lax.fori_loop(0, n // 2, gather_rows, 0)
-    depths = bs[:, width:]
+    depths = bs[:, width:width + z]
+    gb_ref[...] = jnp.sum(bs[:, width + z:], axis=0, keepdims=True)
     b32 = jnp.where(
         kept(total, jnp.concatenate([depths] * (width // z), axis=1)), bs[:, :width], 0.0
     )
     b = b32.astype(BF16)
     inverse, highs, lows = [], [], []
-    cot_sum = jnp.zeros((1, z), F32)
     for i in range(rows):
         inverse.append(1.0 / (EPSILON + jnp.minimum(depths, own_depth[i:i + 1])))
         cot = cot_ref[i].astype(F32)
-        cot_sum = cot_sum + jnp.sum(cot, axis=0, keepdims=True)
         high, low = split(cot * inverse[i])
         highs.append(high)
         lows.append(low)
@@ -197,15 +202,7 @@
         high, low = split(t_of(d))
         gw_part[pl.ds(d, C, stride=C), :] = mm(a_t, jnp.concatenate([high, low], axis=0))
     for p in range(n):
-        pair_w[p % 2, p // 2, :chunk, :] = gw_part[p * chunk:(p + 1) * chunk]
-    sums = jnp.concatenate([cot_sum, jnp.zeros((EXTRA - 1, z), F32)], axis=0)
-
-    def put_sums(m, carry):
-        pair_w[0, m, chunk:, :] = sums
-        pair_w[1, m, chunk:, :] = sums
-        return carry
-
-    lax.fori_loop(0, chips, put_sums, 0)
+        pair_w[p % 2, p // 2] = gw_part[p * chunk:(p + 1) * chunk]
     pair(0, pair_w, got_w).start()
 
     u_high = uhi[...]
@@ -223,13 +220,7 @@
     pair(0, pair_w, got_w).wait_recv()
 
     def join_w(m, carry):
-        both = pair_w[core, m] + got_w[m]
-        high, low = split(both[chunk:chunk + 1])
-        tail = jnp.concatenate(
-            [high.astype(F32), low.astype(F32), jnp.zeros((EXTRA - 2, z), F32)], axis=0
-        )
-        send_w[m, :chunk, :] = both[:chunk].astype(BF16)
-        send_w[m, chunk:, :] = tail.astype(BF16)
+        send_w[m] = (pair_w[core, m] + got_w[m]).astype(BF16)
         return carry
 
     lax.fori_loop(0, chips, join_w, 0)
@@ -255,9 +246,8 @@
     def add_w(m, acc):
         return acc + recv_w[m].astype(F32)
 
-    total_w = lax.fori_loop(0, chips, add_w, jnp.zeros((chunk + EXTRA, z), F32))
-    mine_w[...] = total_w[:chunk].astype(BF16)
-    gb_ref[...] = total_w[chunk:chunk + 1] + total_w[chunk + 1:chunk + 2]
+    total_w = lax.fori_loop(0, chips, add_w, jnp.zeros((chunk, z), F32))
+    mine_w[...] = total_w.astype(BF16)
     gather_start(3, mine_w, all_w)
 
     left_acc = jnp.zeros((rows * samples, C), F32)
@@ -284,7 +274,7 @@
     gr_ref[...] = jnp.where(kept(rows, jnp.broadcast_to(own_depth, (rows, width))), total_r, 0.0)
 
     gather_end(3, all_w)
-    gw_ref[...] = all_w[...].astype(F32)
+    gw_ref[...] = all_w[...]
     gather_sent(0, x_ref, gat)
     gather_sent(3, mine_w, all_w)
     pair(0, pair_w, got_w).wait_send()
@@ -293,36 +283,42 @@
     each(lambda p: across(2, send_r, recv_r, p).wait_send())
 
 
+def finish(*refs):
+    half = len(refs) // 2
+    for source, target in zip(refs[:half], refs[half:]):
+        target[...] = source[...].astype(target.dtype)
+
+
 def local(n, left, right, depth, w_out, bias, pair_cot):
     rows, width = left.shape
     total, z = pair_cot.shape[1:]
     chunk = w_out.shape[0] // n
     vmem = pl.BlockSpec(memory_space=pltpu.VMEM)
-    pu, gl, gr, gw, gb = pl.pallas_call(
+    results = pl.pallas_call(
         functools.partial(kernel, n),
         out_shape=(
             jax.ShapeDtypeStruct((rows, total, z), BF16),
             jax.ShapeDtypeStruct((rows, width), F32),
             jax.ShapeDtypeStruct((rows, width), F32),
-            jax.ShapeDtypeStruct((n, chunk, z), F32),
+            jax.ShapeDtypeStruct((n, chunk, z), BF16),
             jax.ShapeDtypeStruct((1, z), F32),
         ),
         in_specs=[vmem] * 6,
         out_specs=(vmem,) * 5,
         scratch_shapes=[
-            pltpu.VMEM((rows, width + z), BF16),
+            pltpu.VMEM((rows, width + 2 * z), BF16),
             pltpu.VMEM((C * C, z), F32),
             pltpu.VMEM((rows * width, z), F32),
             pltpu.VMEM((C * C, z), F32),
-            pltpu.VMEM((n, rows, width + z), BF16),
-            pltpu.VMEM((total, width + z), F32),
+            pltpu.VMEM((n, rows, width + 2 * z), BF16),
+            pltpu.VMEM((total, width + 2 * z), F32),
             pltpu.VMEM((width, rows * z), BF16),
             pltpu.VMEM((width, rows * z), BF16),
             pltpu.VMEM((rows * width, z), F32),
-            pltpu.VMEM((2, n // 2, chunk + EXTRA, z), F32),
-            pltpu.VMEM((n // 2, chunk + EXTRA, z), F32),
-            pltpu.VMEM((n // 2, chunk + EXTRA, z), BF16),
-            pltpu.VMEM((n // 2, chunk + EXTRA, z), BF16),
+            pltpu.VMEM((2, n // 2, chunk, z), F32),
+            pltpu.VMEM((n // 2, chunk, z), F32),
+            pltpu.VMEM((n // 2, chunk, z), BF16),
+            pltpu.VMEM((n // 2, chunk, z), BF16),
             pltpu.VMEM((total, width), F32),
             pltpu.VMEM((2, n // 2, rows, width), F32),
             pltpu.VMEM((n // 2, rows, width), F32),
@@ -335,6 +331,14 @@
         ],
         compiler_params=pltpu.CompilerParams(collective_id=0, has_side_effects=True),
     )(left, right, depth[None, :], pair_cot, w_out, bias[None, :])
+    pu, gl, gr, gw, gb = pl.pallas_call(
+        finish,
+        out_shape=tuple(
+            jax.ShapeDtypeStruct(r.shape, F32 if k == 3 else r.dtype) for k, r in enumerate(results)
+        ),
+        in_specs=[vmem] * 5,
+        out_specs=(vmem,) * 5,
+    )(*results)
     return pu, gl, gr, gw.reshape(C * C, z), gb.reshape(z)
 
 

time: 35.8 us -> 31.4 us (0.88)
  local copies, waits for them, and re-layouts: 5.2 us -> 0 us
  Pallas kernels: 29.6 us -> 30.6 us
    unnamed x11 -> x0, local copies, waits for them, and re-layouts: 5.2 us -> none
    pallas_call x0 -> x1, Pallas kernels: none -> 1.83 us  [local(): pl.pallas_call(finish, out_shape=tuple((jax.ShapeDtypeStruct(r.shape, F32...]
    pallas_call x1, Pallas kernels: 29.6 us -> 28.7 us  [local(): pl.pallas_call(functools.partial(kernel, n), out_shape=(jax.ShapeDtypeStr...]
where the time goes in v4:
time: 31.4 us; the launch traced here: 31.2 us
  Pallas kernels  30.6 us (97%)
  between operations  0.64 us (2%)
    pallas_call x1, Pallas kernels, local(): pl.pallas_call(functools.partial(kernel, n), out_shape=(jax.ShapeDtypeStr...  28.7 us
    pallas_call x1, Pallas kernels, local(): pl.pallas_call(finish, out_shape=tuple((jax.ShapeDtypeStruct(r.shape, F32...  1.83 us

profile of v4, /device:TPU:1, one launch (start us, length us, event | category | flops | bytes accessed | tf_op | source)
XLA Modules:
  0.0 31.2 jit_solution(58958957284767784)
XLA Ops:
  0.6 28.7 %shard_map.101 = (bf16[4,64,128]{2,1,0:T(8,128)(2,1)}, f32[4,1024]{1,0:T(4,128)}, f32[4,1024]{1,0:T(4,128)}, bf16[16,64,128]{2,1,0:T(8,128)(2,1)}, f32[1,128]{1,0:T(1,128)}) custom-call(bf16[4,1024]{1,0:T(4,128)(2,1)} %left_ref.1, bf16[4,1024]{1,0:T(4,128)(2,1)} %right_ref.1, s32[1,4]{1,0:T(1,128)} %bitcast.4, bf16[4,64,128]{2,1,0:T(8,128)(2,1)} %cot_ref.1, ...), custom_call_target="tpu_custom_call" | custom-call | tf_op jit(solution)/shard_map/pallas_call | solution.py:297
  29.4 1.8 %shard_map.102 = (bf16[4,64,128]{2,1,0:T(8,128)(2,1)}, f32[4,1024]{1,0:T(4,128)}, f32[4,1024]{1,0:T(4,128)}, f32[16,64,128]{2,1,0:T(8,128)}, f32[1,128]{1,0:T(1,128)}) custom-call(bf16[4,64,128]{2,1,0:T(8,128)(2,1)} %get-tuple-element.15.refs_0_, f32[4,1024]{1,0:T(4,128)} %get-tuple-element.16.refs_1_, f32[4,1024]{1,0:T(4,128)} %get-tuple-element.17.refs_2_, ...), custom_call_target="tpu_custom_call" | custom-call | tf_op jit(solution)/shard_map/pallas_call | solution.py:334
